TPU v7x, 32 devices: a whole 2x2x4 slice. The times are simulated.
32 devices in a mesh: dp: 8 (over z, y), tensor: 4 (over x, core).
Axes of the slice: x: 2, y: 2, z: 4, core: 2. Of those that a mesh axis runs over, the one named last changes fastest.
Arguments:
- tokens: bfloat16 [3, 4096, 1536], P(None, ('dp', 'tensor')), may hold values from -6 to 6
- lengths: int32 [3, 32, 6], P(None, ('dp', 'tensor')), may hold values from 1 to 64, 128 in all within a row
- first_gain: bfloat16 [1536], P(('dp', 'tensor')), may hold values from 0.099609375 to 1.8984375
- query_weight: bfloat16 [1536, 1536], P(('dp', 'tensor')), may hold values from -0.15625 to 0.15625
- key_weight: bfloat16 [1536, 768], P(('dp', 'tensor')), may hold values from -0.15625 to 0.15625
- value_weight: bfloat16 [1536, 768], P(('dp', 'tensor')), may hold values from -0.15625 to 0.15625
- output_weight: bfloat16 [1536, 1536], P(('dp', 'tensor')), may hold values from -0.4375 to 0.4375
- second_gain: bfloat16 [1536], P(('dp', 'tensor')), may hold values from 0.099609375 to 1.8984375
- gate_weight: bfloat16 [1536, 4096], P('dp', 'tensor'), may hold values from -0.15625 to 0.15625
- up_weight: bfloat16 [1536, 4096], P('dp', 'tensor'), may hold values from -0.15625 to 0.15625
- down_weight: bfloat16 [4096, 1536], P('tensor', 'dp'), may hold values from -0.09375 to 0.09375
- cotangent: bfloat16 [3, 4096, 1536], P(None, ('dp', 'tensor')), may hold values from -6 to 6
Outputs:
- layer_out: bfloat16 [3, 4096, 1536], P(None, ('dp', 'tensor'))
- input_grad: float32 [3, 4096, 1536], P(None, ('dp', 'tensor'))
- first_gain_grad: float32 [1536], P(('dp', 'tensor'))
- query_grad: float32 [1536, 1536], P(('dp', 'tensor'))
- key_grad: float32 [1536, 768], P(('dp', 'tensor'))
- value_grad: float32 [1536, 768], P(('dp', 'tensor'))
- output_grad: float32 [1536, 1536], P(('dp', 'tensor'))
- second_gain_grad: float32 [1536], P(('dp', 'tensor'))
- gate_grad: float32 [1536, 4096], P('dp', 'tensor')
- up_grad: float32 [1536, 4096], P('dp', 'tensor')
- down_grad: float32 [4096, 1536], P('tensor', 'dp')
Inputs may be any that keep to these rules, and one draw needn't show every extreme that they name: Row lengths[m, p] splits the 128 rows of pack p of micro-batch m into 6 runs in order, summing to 128; the first 5 runs are sequences, the last is padding; no run is longer than 64 rows.
All inputs are finite; a program needn't handle non-finite values.
Results may differ from a plain program's by a relative error of at most 0.013.
Values may be sent and summed in bfloat16 or wider, within the bound.
No kernel may reach another device: no remote copies, remote signals or barrier semaphores. Data moves between devices by JAX's collectives and lax.ppermute only.
A program may use at most 192 MiB of HBM per device.

v0:
```python
import math
import jax
import jax.numpy as jnp
from jax import lax
from jax.sharding import PartitionSpec as P

HEADS = 16
KV_HEADS = 8
HEAD = 96
SLOTS = 6
GROUP = HEADS // KV_HEADS
LANES = 128
EPSILON = 1e-05
ROPE_BASE = 100000.0
NEG_LARGE = -1e30
AXES = ("dp", "tensor")
bf16 = jnp.bfloat16
f32 = jnp.float32


def pack_layout(seq_lengths, row_count):
    seq_ends = jnp.cumsum(seq_lengths)
    seq_starts = seq_ends - seq_lengths
    row_index = jnp.arange(row_count, dtype=jnp.int32)
    segment = jnp.sum((row_index[:, None] >= seq_ends[None, :]).astype(jnp.int32), axis=1)
    owner_hot = segment[:, None] == jnp.arange(seq_lengths.shape[0], dtype=jnp.int32)[None, :]
    position = row_index - jnp.sum(jnp.where(owner_hot, seq_starts[None, :], 0), axis=1)
    return (segment, position)


def rotary_tables(position, head_size):
    half_size = head_size // 2
    freq_index = jnp.arange(half_size, dtype=f32)
    inverse = jnp.exp(freq_index * (-2.0 / head_size) * math.log(ROPE_BASE))
    angles = position.astype(f32)[..., None] * inverse
    return (jnp.cos(angles), jnp.sin(angles))


def rotate(vectors, cosine, sine_part):
    half_size = vectors.shape[-1] // 2
    lower_half = vectors[..., :half_size]
    upper_half = vectors[..., half_size:]
    cosine = cosine[..., None, :]
    sine_part = sine_part[..., None, :]
    return jnp.concatenate(
        [
            lower_half * cosine - upper_half * sine_part,
            upper_half * cosine + lower_half * sine_part,
        ],
        axis=-1,
    )


def product(left_side, right_side):
    return jnp.dot(left_side, right_side, preferred_element_type=f32)


def across(left_side, right_side):
    return lax.dot_general(
        left_side, right_side, (((0,), (0,)), ((), ())), preferred_element_type=f32
    )


def against(left_side, right_side):
    return lax.dot_general(
        left_side, right_side, (((1,), (1,)), ((), ())), preferred_element_type=f32
    )


def bits_of(size):
    return [1 << k for k in range(size.bit_length() - 1)]


def near_first(size):
    masks = bits_of(size)
    return masks[:1] + masks[:0:-1]


def far_first(size):
    return bits_of(size)[::-1]


def rel_source(me, masks, block, count):
    place = jnp.arange(count, dtype=jnp.int32)
    step = place // block
    delta = jnp.zeros_like(step)
    for k, mask in enumerate(masks):
        delta = delta + (step >> k & 1) * mask
    return (me ^ delta) * block + place % block


def one_hot(source):
    count = source.shape[0]
    rows = lax.broadcasted_iota(jnp.int32, (count, count), 0)
    return (rows == source[None, :]).astype(bf16)


def join(parts):
    return parts[0] if len(parts) == 1 else jnp.concatenate(parts, axis=0)


def program(sizes):
    dp_n, tp_n = (sizes["dp"], sizes["tensor"])
    world = dp_n * tp_n

    def swap(array, mask):
        return lax.ppermute(array, AXES, [(i, i ^ mask) for i in range(world)])

    def gather(own, masks, loose):
        held = [own]
        for k, mask in enumerate(masks):
            got = [swap(part, mask) for part in held]
            held = held + got
            if k < len(masks) - loose:
                held = [join(held)]
        return held

    def per_device(
        tokens,
        lengths,
        first_gain,
        query_weight,
        key_weight,
        value_weight,
        output_weight,
        second_gain,
        gate_weight,
        up_weight,
        down_weight,
        cotangent,
    ):
        micro, per_pack, width = tokens.shape
        rows = micro * per_pack
        qw, kw = (query_weight.shape[1], key_weight.shape[1])
        ff = gate_weight.shape[1]
        wide = qw + 2 * kw
        shard = query_weight.shape[0]
        dp_i, t_i = (lax.axis_index("dp"), lax.axis_index("tensor"))
        me = dp_i * tp_n + t_i
        dp_attn = [m * tp_n for m in near_first(dp_n)]
        t_bits = bits_of(tp_n)[::-1]
        attn_masks = dp_attn + t_bits
        mlp_masks = [m * tp_n for m in far_first(dp_n)]
        x_low = tokens.reshape(rows, width)
        dy_low = cotangent.reshape(rows, width)
        gains = jnp.pad(jnp.stack([first_gain, second_gain], axis=1), ((0, 0), (0, LANES - 2)))
        own_qkv = jnp.concatenate([query_weight, key_weight, value_weight, gains], axis=1)
        own_gu = jnp.concatenate([gate_weight, up_weight], axis=1)
        own_down = down_weight.T

        def gather_attn(own):
            held = gather(own, dp_attn, 2)
            far = [swap(part, t_bits[0]) for part in held]
            pieces = [join(held), join(far)]
            for mask in t_bits[1:]:
                pieces = pieces + [swap(part, mask) for part in pieces]
            return pieces

        qkv_pieces = gather_attn(own_qkv)
        out_pieces = gather_attn(output_weight)
        gu_full = join(gather(own_gu, mlp_masks, 3))
        down_full = join(gather(own_down, mlp_masks, 3))
        n_pieces = len(qkv_pieces)
        part = width // n_pieces
        pick_attn = one_hot(rel_source(me, attn_masks, shard, width))
        mlp_source = rel_source(dp_i, [m // tp_n for m in mlp_masks], shard * tp_n, width)
        pick_mlp = one_hot(mlp_source)

        def order(array, pick):
            return product(array, pick).astype(bf16)

        def restore(array, pick):
            return against(array, pick)

        gains_rel = jnp.concatenate([piece[:, wide : wide + 2] for piece in qkv_pieces], axis=0)
        g1_rel = gains_rel[:, 0].astype(f32)
        g2 = restore(gains_rel[:, 1][None, :], pick_attn)[0]
        segment, position = jax.vmap(lambda own: pack_layout(own, per_pack))(lengths[:, 0])
        cosine, sine_part = rotary_tables(position, HEAD)
        row_index = jnp.arange(per_pack, dtype=jnp.int32)
        allowed = (
            (segment[:, :, None] == segment[:, None, :])
            & (row_index[None, None, :] <= row_index[None, :, None])
            & (segment < SLOTS - 1)[:, :, None]
        )[:, None, None]
        factor = 1.0 / math.sqrt(HEAD)
        inputs = x_low.astype(f32)
        r1 = lax.rsqrt(jnp.mean(inputs * inputs, axis=1, keepdims=True) + EPSILON)
        x_rel = order(x_low, pick_attn).astype(f32)
        n1_rel = (x_rel * r1 * g1_rel).astype(bf16)
        n1_parts = [n1_rel[:, k * part : (k + 1) * part] for k in range(n_pieces)]
        qkv = sum((product(a, b) for a, b in zip(n1_parts, qkv_pieces)))
        shape = (micro, per_pack)
        queries = rotate(qkv[:, :qw].reshape(shape + (HEADS, HEAD)), cosine, sine_part)
        queries = queries.astype(bf16).reshape(shape + (KV_HEADS, GROUP, HEAD))
        keys = rotate(
            qkv[:, qw : qw + kw].reshape(shape + (KV_HEADS, HEAD)), cosine, sine_part
        ).astype(bf16)
        values = qkv[:, qw + kw : wide].astype(bf16).reshape(shape + (KV_HEADS, HEAD))
        scores = jnp.einsum("pqhgd,pkhd->phgqk", queries, keys, preferred_element_type=f32) * factor
        row_peak = jnp.max(jnp.where(allowed, scores, NEG_LARGE), axis=-1, keepdims=True)
        raised = jnp.where(allowed, jnp.exp(jnp.where(allowed, scores - row_peak, 0.0)), 0.0)
        totals = jnp.sum(raised, axis=-1, keepdims=True)
        probs = raised / jnp.where(totals > 0, totals, 1.0)
        probs_low = probs.astype(bf16)
        attended = jnp.einsum("phgqk,pkhd->pqhgd", probs_low, values, preferred_element_type=f32)
        attended = attended.reshape(rows, qw).astype(bf16)
        att_rel = order(attended, pick_attn)
        att_parts = [att_rel[:, k * part : (k + 1) * part] for k in range(n_pieces)]
        middle = inputs + sum((product(a, b) for a, b in zip(att_parts, out_pieces)))
        r2 = lax.rsqrt(jnp.mean(middle * middle, axis=1, keepdims=True) + EPSILON)
        n2 = (middle * r2 * g2).astype(bf16)
        n2_rel = order(n2, pick_mlp)
        dy_rel = order(dy_low, pick_mlp)

        def spread(own):
            return join(gather(own, t_bits, tp_n))

        def collect(partial):
            for mask in t_bits[::-1]:
                half = partial.shape[0] // 2
                got = swap(partial[half:].astype(bf16), mask)
                partial = partial[:half].astype(f32) + got.astype(f32)
            return partial

        dy_all = spread(dy_rel)
        n2_all = spread(n2_rel)
        gu = product(n2_all, gu_full)
        gate, up = (gu[:, :ff], gu[:, ff:])
        sig = jax.nn.sigmoid(gate)
        hidden = (gate * sig * up).astype(bf16)
        dhid = product(dy_all, down_full)
        dgate = (dhid * up * sig * (1.0 + gate * (1.0 - sig))).astype(bf16)
        dup = (dhid * gate * sig).astype(bf16)
        dgu = jnp.concatenate([dgate, dup], axis=1)
        dn2 = restore(collect(against(dgu, gu_full).astype(bf16)).astype(bf16), pick_mlp)
        down_sum = collect(against(hidden, down_full).astype(bf16)).astype(bf16)
        layer_out = (middle + restore(down_sum, pick_mlp)).astype(bf16)

        def reduce_rows(own_half, sent_half, masks):
            total = own_half() + swap(sent_half().astype(bf16), masks[0]).astype(f32)
            for mask in masks[1:]:
                half = total.shape[0] // 2
                got = swap(total[half:].astype(bf16), mask)
                total = total[:half] + got.astype(f32)
            return total

        half = width // 2

        def mlp_grad(left, right):
            return reduce_rows(
                lambda: across(left[:, :half], right),
                lambda: across(left[:, half:], right),
                mlp_masks[::-1],
            )

        down_grad = mlp_grad(dy_all, hidden).T
        gate_grad = mlp_grad(n2_all, dgate)
        up_grad = mlp_grad(n2_all, dup)
        dy = dy_low.astype(f32)
        weighted = dn2 * g2
        dmid = (
            dy
            + r2 * weighted
            - middle * (r2 * r2 * r2) * jnp.mean(weighted * middle, axis=1, keepdims=True)
        )
        dmb = dmid.astype(bf16)

        def attn_grad(lefts, right):
            held = [across(left, right) for left in lefts]
            for mask in t_bits[1:][::-1]:
                n = len(held) // 2
                got = [swap(piece.astype(bf16), mask) for piece in held[n:]]
                held = [a + b.astype(f32) for a, b in zip(held[:n], got)]
            return reduce_rows(lambda: held[0], lambda: held[1], [t_bits[0]] + dp_attn[::-1])

        output_grad = attn_grad(att_parts, dmb)
        datt_rel = jnp.concatenate([against(dmb, piece) for piece in out_pieces], axis=1)
        datt = restore(datt_rel.astype(bf16), pick_attn).astype(bf16)
        datt = datt.reshape(shape + (KV_HEADS, GROUP, HEAD))
        dprob = jnp.einsum("pqhgd,pkhd->phgqk", datt, values, preferred_element_type=f32)
        delta = jnp.sum(probs * dprob, axis=-1, keepdims=True)
        dscore = (probs * (dprob - delta)).astype(bf16)
        dvalue = jnp.einsum("phgqk,pqhgd->pkhd", probs_low, datt, preferred_element_type=f32)
        dqr = jnp.einsum("phgqk,pkhd->pqhgd", dscore, keys, preferred_element_type=f32) * factor
        dkr = jnp.einsum("phgqk,pqhgd->pkhd", dscore, queries, preferred_element_type=f32) * factor
        dq = rotate(dqr.reshape(shape + (HEADS, HEAD)), cosine, -sine_part)
        dk = rotate(dkr, cosine, -sine_part)
        dqkv = jnp.concatenate(
            [
                dq.astype(bf16).reshape(rows, qw),
                dk.astype(bf16).reshape(rows, kw),
                dvalue.astype(bf16).reshape(rows, kw),
            ],
            axis=1,
        )
        qkv_grad = attn_grad(n1_parts, dqkv)
        dn1_rel = jnp.concatenate([against(dqkv, piece[:, :wide]) for piece in qkv_pieces], axis=1)
        weighted = dn1_rel * g1_rel
        part_rel = r1 * weighted - x_rel * (r1 * r1 * r1) * jnp.mean(
            weighted * x_rel, axis=1, keepdims=True
        )
        high = part_rel.astype(bf16)
        low = (part_rel - high.astype(f32)).astype(bf16)
        input_grad = dmid + restore(high, pick_attn) + restore(low, pick_attn)
        own_wide = own_qkv[:, :wide].astype(f32)
        first_gain_grad = jnp.sum(own_wide * qkv_grad, axis=1) / first_gain.astype(f32)
        second = jnp.sum(
            gate_weight.astype(f32) * gate_grad + up_weight.astype(f32) * up_grad, axis=1
        )
        second = lax.psum(second, "tensor")
        second = lax.dynamic_slice(second, (t_i * shard,), (shard,))
        second_gain_grad = second / second_gain.astype(f32)
        return (
            layer_out.reshape(tokens.shape),
            input_grad.reshape(tokens.shape),
            first_gain_grad,
            qkv_grad[:, :qw],
            qkv_grad[:, qw : qw + kw],
            qkv_grad[:, qw + kw :],
            output_grad,
            second_gain_grad,
            gate_grad,
            up_grad,
            down_grad,
        )

    return per_device


def solution(mesh):
    rows = P(None, AXES, None)
    split = P(AXES, None)
    placed = (
        rows,
        rows,
        P(AXES),
        split,
        split,
        split,
        split,
        P(AXES),
        P("dp", "tensor"),
        P("dp", "tensor"),
        P("tensor", "dp"),
        rows,
    )
    return jax.shard_map(
        program(dict(mesh.shape)),
        mesh=mesh,
        in_specs=placed,
        out_specs=(
            rows,
            rows,
            P(AXES),
            split,
            split,
            split,
            split,
            P(AXES),
            P("dp", "tensor"),
            P("dp", "tensor"),
            P("tensor", "dp"),
        ),
        check_vma=False,
    )
```

profile of v0, /device:TPU:0, one launch (start us, length us, event | category | flops | bytes accessed | tf_op | source)
XLA Modules:
  0.0 805.7 jit_solution(15397457779507763800)
XLA Ops:
  29.8 8.6 %collective-permute-done.4 = bf16[96,3200]{1,0:T(8,128)(2,1)S(1)} collective-permute-done((bf16[96,3200]{1,0:T(8,128)(2,1)S(1)}, bf16[96,3200]{1,0:T(8,128)(2,1)S(1)}, u32[]{:S(2)}, u32[]{:S(2)}) %collective-permute-start.4) | collective-permute-done | bytes 614432 | tf_op jit(solution)/shard_map/ppermute | solution.py:107
  39.7 27.5 %collective-permute-done.1 = bf16[96,3200]{1,0:T(8,128)(2,1)S(1)} collective-permute-done((bf16[96,3200]{1,0:T(8,128)(2,1)S(1)}, bf16[96,3200]{1,0:T(8,128)(2,1)S(1)}, u32[]{:S(2)}, u32[]{:S(2)}) %collective-permute-start.1) | collective-permute-done | bytes 614432 | tf_op jit(solution)/shard_map/ppermute | solution.py:107
  76.1 8.4 %collective-permute-done.3 = bf16[96,3200]{1,0:T(8,128)(2,1)S(1)} collective-permute-done((bf16[96,3200]{1,0:T(8,128)(2,1)S(1)}, bf16[96,3200]{1,0:T(8,128)(2,1)S(1)}, u32[]{:S(2)}, u32[]{:S(2)}) %collective-permute-start.3) | collective-permute-done | bytes 614432 | tf_op jit(solution)/shard_map/ppermute | solution.py:107
  88.3 13.0 %collective-permute-done.6 = bf16[96,3200]{1,0:T(8,128)(2,1)S(1)} collective-permute-done((bf16[96,3200]{1,0:T(8,128)(2,1)S(1)}, bf16[96,3200]{1,0:T(8,128)(2,1)S(1)}, u32[]{:S(2)}, u32[]{:S(2)}) %collective-permute-start.6) | collective-permute-done | bytes 614432 | tf_op jit(solution)/shard_map/ppermute | solution.py:107
  102.2 9.9 %collective-permute-done.7 = bf16[96,3200]{1,0:T(8,128)(2,1)S(1)} collective-permute-done((bf16[96,3200]{1,0:T(8,128)(2,1)S(1)}, bf16[96,3200]{1,0:T(8,128)(2,1)S(1)}, u32[]{:S(2)}, u32[]{:S(2)}) %collective-permute-start.7) | collective-permute-done | bytes 614432 | tf_op jit(solution)/shard_map/ppermute | solution.py:107
  141.3 7.3 collective-permute-done.34
  149.2 23.1 %collective-permute-done.23 = bf16[192,2048]{1,0:T(8,128)(2,1)S(1)} collective-permute-done((bf16[192,2048]{1,0:T(8,128)(2,1)}, bf16[192,2048]{1,0:T(8,128)(2,1)S(1)}, u32[]{:S(2)}, u32[]{:S(2)}) %collective-permute-start.23) | collective-permute-done | bytes 786464 | tf_op jit(solution)/shard_map/ppermute | solution.py:107
  254.1 18.8 %collective-permute-done.36 = bf16[192,1024]{1,0:T(8,128)(2,1)S(1)} collective-permute-done((bf16[192,1024]{1,0:T(8,128)(2,1)S(1)}, bf16[192,1024]{1,0:T(8,128)(2,1)S(1)}, u32[]{:S(2)}, u32[]{:S(2)}) %collective-permute-start.36) | collective-permute-done | bytes 393248 | tf_op jit(solution)/shard_map/ppermute | solution.py:107
  280.2 13.4 %collective-permute-done.28 = bf16[192,2048]{1,0:T(8,128)(2,1)S(1)} collective-permute-done((bf16[192,2048]{1,0:T(8,128)(2,1)}, bf16[192,2048]{1,0:T(8,128)(2,1)S(1)}, u32[]{:S(2)}, u32[]{:S(2)}) %collective-permute-start.28) | collective-permute-done | bytes 786464 | tf_op jit(solution)/shard_map/ppermute | solution.py:107
  295.1 13.2 %collective-permute-done.29 = bf16[192,2048]{1,0:T(8,128)(2,1)S(1)} collective-permute-done((bf16[192,2048]{1,0:T(8,128)(2,1)S(1)}, bf16[192,2048]{1,0:T(8,128)(2,1)S(1)}, u32[]{:S(2)}, u32[]{:S(2)}) %collective-permute-start.29) | collective-permute-done | bytes 786464 | tf_op jit(solution)/shard_map/ppermute | solution.py:107
  314.0 16.8 %fusion.176 = f32[1536,2048]{1,0:T(8,128)} fusion(bf16[1536,2048]{1,0:T(8,128)(2,1)S(1)} %copy-done.68, bf16[384,1536]{1,0:T(8,128)(2,1)S(1)} %collective-permute-done.22, bf16[384,1536]{1,0:T(8,128)(2,1)S(1)} %collective-permute-done.21, bf16[384,1536]{1,0:T(8,128)(2,1)S(1)} %collective-permute-done.20, bf16[384,1536]{1,0:T(8,128)(2,1)S(1)} %fusion.47), kind=kOutput, calls=%fused_computation.319 | convolution fusion | flops 9682550784 | bytes 23592960 | tf_op jit(solution)/shard_map/dot_general | solution.py:55
  330.8 15.0 %multiply_convert_fusion.1 = (bf16[1536,1024]{1,0:T(8,128)(2,1)S(1)}, bf16[1536,1024]{1,0:T(8,128)(2,1)}, bf16[1536,1024]{1,0:T(8,128)(2,1)}) fusion(f32[1536,2048]{1,0:T(8,128)} %fusion.176, bf16[1536,1024]{1,0:T(8,128)(2,1)} %constant_dynamic-update-slice_fusion.31, bf16[384,1536]{1,0:T(8,128)(2,1)} %copy-done.42, bf16[384,1536]{1,0:T(8,128)(2,1)} %copy-done.41, ...), kind=kOutput, calls=%fused_computation.19 | convolution fusion | flops 4875878400 | bytes 29884416 | tf_op jit(solution)/shard_map/dot_general | solution.py:55
  345.8 6.8 fusion.92
  359.8 15.1 %convolution_convert_fusion.1 = bf16[1536,1536]{1,0:T(8,128)(2,1)} fusion(bf16[1536,2048]{1,0:T(8,128)(2,1)} %constant_dynamic-update-slice_fusion.22, bf16[1536,1024]{1,0:T(8,128)(2,1)} %get-tuple-element.19, bf16[1536,1024]{1,0:T(8,128)(2,1)S(1)} %get-tuple-element.18), kind=kOutput, calls=%fused_computation.14 | convolution fusion | flops 9678618624 | bytes 17301504 | tf_op jit(solution)/shard_map/dot_general | solution.py:65
  379.3 7.4 convolution_convert_fusion
  396.0 28.0 %collective-permute-done.59 = bf16[768,1024]{1,0:T(8,128)(2,1)} collective-permute-done((bf16[768,1024]{1,0:T(8,128)(2,1)}, bf16[768,1024]{1,0:T(8,128)(2,1)}, u32[]{:S(2)}, u32[]{:S(2)}) %collective-permute-start.59) | collective-permute-done | bytes 1572896 | tf_op jit(solution)/shard_map/ppermute | solution.py:107
  429.7 24.8 %collective-permute-done.56 = bf16[768,1024]{1,0:T(8,128)(2,1)S(1)} collective-permute-done((bf16[768,1024]{1,0:T(8,128)(2,1)}, bf16[768,1024]{1,0:T(8,128)(2,1)S(1)}, u32[]{:S(2)}, u32[]{:S(2)}) %collective-permute-start.56) | collective-permute-done | bytes 1572896 | tf_op jit(solution)/shard_map/ppermute | solution.py:107
  463.5 22.9 %collective-permute-done.57 = bf16[384,1024]{1,0:T(8,128)(2,1)S(1)} collective-permute-done((bf16[384,1024]{1,0:T(8,128)(2,1)S(1)}, bf16[384,1024]{1,0:T(8,128)(2,1)S(1)}, u32[]{:S(2)}, u32[]{:S(2)}) %collective-permute-start.57) | collective-permute-done | bytes 786464 | tf_op jit(solution)/shard_map/ppermute | solution.py:107
  496.8 9.9 %collective-permute-done.61 = bf16[192,1024]{1,0:T(8,128)(2,1)S(1)} collective-permute-done((bf16[192,1024]{1,0:T(8,128)(2,1)S(1)}, bf16[192,1024]{1,0:T(8,128)(2,1)S(1)}, u32[]{:S(2)}, u32[]{:S(2)}) %collective-permute-start.61) | collective-permute-done | bytes 393248 | tf_op jit(solution)/shard_map/ppermute | solution.py:107
  512.9 29.6 %psum.7 = f32[192]{0:T(256)} all-reduce(f32[192]{0:T(256)} %get-tuple-element.11), channel_id=1, replica_groups=mesh['dp'=8,'tensor'=4] {'tensor'}, use_global_device_ids=true, to_apply=%region_12.13 | all-reduce | flops 192 | bytes 1536 | tf_op jit(solution)/shard_map/psum | solution.py:311
  649.9 69.7 %collective-permute-done.52 = bf16[384,1536]{1,0:T(8,128)(2,1)S(1)} collective-permute-done((bf16[384,1536]{1,0:T(8,128)(2,1)S(1)}, bf16[384,1536]{1,0:T(8,128)(2,1)S(1)}, u32[]{:S(2)}, u32[]{:S(2)}) %collective-permute-start.52) | collective-permute-done | bytes 1179680 | tf_op jit(solution)/shard_map/ppermute | solution.py:107
  739.2 27.2 %collective-permute-done.47 = bf16[192,3072]{1,0:T(8,128)(2,1)S(1)} collective-permute-done((bf16[192,3072]{1,0:T(8,128)(2,1)S(1)}, bf16[192,3072]{1,0:T(8,128)(2,1)S(1)}, u32[]{:S(2)}, u32[]{:S(2)}) %collective-permute-start.47) | collective-permute-done | bytes 1179680 | tf_op jit(solution)/shard_map/ppermute | solution.py:107
  773.4 20.7 %collective-permute-done.48 = bf16[96,3072]{1,0:T(8,128)(2,1)S(1)} collective-permute-done((bf16[96,3072]{1,0:T(8,128)(2,1)S(1)}, bf16[96,3072]{1,0:T(8,128)(2,1)S(1)}, u32[]{:S(2)}, u32[]{:S(2)}) %collective-permute-start.48) | collective-permute-done | bytes 589856 | tf_op jit(solution)/shard_map/ppermute | solution.py:107
  796.6 6.7 collective-permute-done.49
  (471 shorter events, 359.3 us)
Async XLA Ops:
  0.7 112.3 %collective-permute-start.30 = (bf16[192,1024]{1,0:T(8,128)(2,1)}, bf16[192,1024]{1,0:T(8,128)(2,1)}, u32[]{:S(2)}, u32[]{:S(2)}) collective-permute-start(bf16[192,1024]{1,0:T(8,128)(2,1)} %bitcast.152), channel_id=1, source_target_pairs={{0,16},{1,17},{2,18},{3,19},{4,20},{5,21},{6,22},{7,23},{8,24},{9,... | collective-permute-start | bytes 1179656 | tf_op jit(solution)/shard_map/ppermute | solution.py:107
  4.8 109.7 %collective-permute-start.31 = (bf16[192,1024]{1,0:T(8,128)(2,1)}, bf16[192,1024]{1,0:T(8,128)(2,1)}, u32[]{:S(2)}, u32[]{:S(2)}) collective-permute-start(bf16[192,1024]{1,0:T(8,128)(2,1)} %bitcast.153), channel_id=1, source_target_pairs={{0,8},{1,9},{2,10},{3,11},{4,12},{5,13},{6,14},{7,15},{8,0},{9,1},... | collective-permute-start | bytes 1179656 | tf_op jit(solution)/shard_map/ppermute | solution.py:107
  26.1 90.0 %collective-permute-start.11 = (bf16[96,1536]{1,0:T(8,128)(2,1)}, bf16[96,1536]{1,0:T(8,128)(2,1)S(1)}, u32[]{:S(2)}, u32[]{:S(2)}) collective-permute-start(bf16[96,1536]{1,0:T(8,128)(2,1)} %get-tuple-element.42), channel_id=1, source_target_pairs={{0,16},{1,17},{2,18},{3,19},{4,20},{5,21},{6,22},{7,23},{8,24},{9,... | collective-permute-start | bytes 884744 | tf_op jit(solution)/shard_map/ppermute | solution.py:107
  112.1 65.9 %collective-permute-start.8 = (bf16[384,3200]{1,0:T(8,128)(2,1)}, bf16[384,3200]{1,0:T(8,128)(2,1)}, u32[]{:S(2)}, u32[]{:S(2)}) collective-permute-start(bf16[384,3200]{1,0:T(8,128)(2,1)} %constant_dynamic-update-slice_fusion), channel_id=1, source_target_pairs={{0,1},{1,0},{2,3},{3,2},{4,5},{5,4},{6,7},{7,6},{8,9},{9,8},{10,11... | collective-permute-start | bytes 7372808 | tf_op jit(solution)/shard_map/ppermute | solution.py:107
  112.9 66.1 %collective-permute-start.9 = (bf16[384,3200]{1,0:T(8,128)(2,1)}, bf16[384,3200]{1,0:T(8,128)(2,1)}, u32[]{:S(2)}, u32[]{:S(2)}) collective-permute-start(bf16[384,3200]{1,0:T(8,128)(2,1)} %constant_dynamic-update-slice_fusion.5), channel_id=1, source_target_pairs={{0,1},{1,0},{2,3},{3,2},{4,5},{5,4},{6,7},{7,6},{8,9},{9,8},{10,11... | collective-permute-start | bytes 7372808 | tf_op jit(solution)/shard_map/ppermute | solution.py:107
  141.3 104.0 %collective-permute-start.24 = (bf16[192,2048]{1,0:T(8,128)(2,1)}, bf16[192,2048]{1,0:T(8,128)(2,1)}, u32[]{:S(2)}, u32[]{:S(2)}) collective-permute-start(bf16[192,2048]{1,0:T(8,128)(2,1)} %get-tuple-element.35), channel_id=1, source_target_pairs={{0,8},{1,9},{2,10},{3,11},{4,12},{5,13},{6,14},{7,15},{8,0},{9,1},... | collective-permute-start | bytes 2359304 | tf_op jit(solution)/shard_map/ppermute | solution.py:107
  172.3 74.5 %collective-permute-start.26 = (bf16[192,2048]{1,0:T(8,128)(2,1)}, bf16[192,2048]{1,0:T(8,128)(2,1)}, u32[]{:S(2)}, u32[]{:S(2)}) collective-permute-start(bf16[192,2048]{1,0:T(8,128)(2,1)} %get-tuple-element.35), channel_id=1, source_target_pairs={{0,4},{1,5},{2,6},{3,7},{4,0},{5,1},{6,2},{7,3},{8,12},{9,13},{10,... | collective-permute-start | bytes 2359304 | tf_op jit(solution)/shard_map/ppermute | solution.py:107
  174.7 100.4 %collective-permute-start.39 = (bf16[384,1536]{1,0:T(8,128)(2,1)}, bf16[384,1536]{1,0:T(8,128)(2,1)}, u32[]{:S(2)}, u32[]{:S(2)}) collective-permute-start(bf16[384,1536]{1,0:T(8,128)(2,1)} %fusion.57), channel_id=1, source_target_pairs={{0,2},{1,3},{2,0},{3,1},{4,6},{5,7},{6,4},{7,5},{8,10},{9,11},{10,... | collective-permute-start | bytes 3538952 | tf_op jit(solution)/shard_map/ppermute | solution.py:107
  178.0 58.2 %collective-permute-start.18 = (bf16[384,1536]{1,0:T(8,128)(2,1)}, bf16[384,1536]{1,0:T(8,128)(2,1)}, u32[]{:S(2)}, u32[]{:S(2)}) collective-permute-start(bf16[384,1536]{1,0:T(8,128)(2,1)} %constant_dynamic-update-slice_fusion.11), channel_id=1, source_target_pairs={{0,1},{1,0},{2,3},{3,2},{4,5},{5,4},{6,7},{7,6},{8,9},{9,8},{10,11... | collective-permute-start | bytes 3538952 | tf_op jit(solution)/shard_map/ppermute | solution.py:107
  179.1 59.8 %collective-permute-start.19 = (bf16[384,1536]{1,0:T(8,128)(2,1)}, bf16[384,1536]{1,0:T(8,128)(2,1)}, u32[]{:S(2)}, u32[]{:S(2)}) collective-permute-start(bf16[384,1536]{1,0:T(8,128)(2,1)} %constant_dynamic-update-slice_fusion.16), channel_id=1, source_target_pairs={{0,1},{1,0},{2,3},{3,2},{4,5},{5,4},{6,7},{7,6},{8,9},{9,8},{10,11... | collective-permute-start | bytes 3538952 | tf_op jit(solution)/shard_map/ppermute | solution.py:107
  249.6 44.0 %collective-permute-start.20 = (bf16[384,1536]{1,0:T(8,128)(2,1)S(1)}, bf16[384,1536]{1,0:T(8,128)(2,1)S(1)}, u32[]{:S(2)}, u32[]{:S(2)}) collective-permute-start(bf16[384,1536]{1,0:T(8,128)(2,1)S(1)} %fusion.47), channel_id=1, source_target_pairs={{0,2},{1,3},{2,0},{3,1},{4,6},{5,7},{6,4},{7,5},{8,10},{9,11},{10,... | collective-permute-start | bytes 3538952 | tf_op jit(solution)/shard_map/ppermute | solution.py:107
  358.3 65.7 %collective-permute-start.59 = (bf16[768,1024]{1,0:T(8,128)(2,1)}, bf16[768,1024]{1,0:T(8,128)(2,1)}, u32[]{:S(2)}, u32[]{:S(2)}) collective-permute-start(bf16[768,1024]{1,0:T(8,128)(2,1)} %fusion.89), channel_id=1, source_target_pairs={{0,4},{1,5},{2,6},{3,7},{4,0},{5,1},{6,2},{7,3},{8,12},{9,13},{10,... | collective-permute-start | bytes 4718600 | tf_op jit(solution)/shard_map/ppermute | solution.py:107
  378.7 75.8 %collective-permute-start.56 = (bf16[768,1024]{1,0:T(8,128)(2,1)}, bf16[768,1024]{1,0:T(8,128)(2,1)S(1)}, u32[]{:S(2)}, u32[]{:S(2)}) collective-permute-start(bf16[768,1024]{1,0:T(8,128)(2,1)} %fusion.86), channel_id=1, source_target_pairs={{0,4},{1,5},{2,6},{3,7},{4,0},{5,1},{6,2},{7,3},{8,12},{9,13},{10,... | collective-permute-start | bytes 4718600 | tf_op jit(solution)/shard_map/ppermute | solution.py:107
  386.8 100.3 %collective-permute-start.42 = (bf16[768,1536]{1,0:T(8,128)(2,1)S(1)}, bf16[768,1536]{1,0:T(8,128)(2,1)}, u32[]{:S(2)}, u32[]{:S(2)}) collective-permute-start(bf16[768,1536]{1,0:T(8,128)(2,1)S(1)} %slice.327), channel_id=1, source_target_pairs={{0,1},{1,0},{2,3},{3,2},{4,5},{5,4},{6,7},{7,6},{8,9},{9,8},{10,11... | collective-permute-start | bytes 7077896 | tf_op jit(solution)/shard_map/ppermute | solution.py:107
  387.1 104.6 %collective-permute-start.37 = (bf16[768,1536]{1,0:T(8,128)(2,1)S(1)}, bf16[768,1536]{1,0:T(8,128)(2,1)}, u32[]{:S(2)}, u32[]{:S(2)}) collective-permute-start(bf16[768,1536]{1,0:T(8,128)(2,1)S(1)} %slice.323), channel_id=1, source_target_pairs={{0,1},{1,0},{2,3},{3,2},{4,5},{5,4},{6,7},{7,6},{8,9},{9,8},{10,11... | collective-permute-start | bytes 7077896 | tf_op jit(solution)/shard_map/ppermute | solution.py:107
  394.6 64.4 %collective-permute-start.63 = (bf16[384,1024]{1,0:T(8,128)(2,1)S(1)}, bf16[384,1024]{1,0:T(8,128)(2,1)S(1)}, u32[]{:S(2)}, u32[]{:S(2)}) collective-permute-start(bf16[384,1024]{1,0:T(8,128)(2,1)S(1)} %slice.497), channel_id=1, source_target_pairs={{0,8},{1,9},{2,10},{3,11},{4,12},{5,13},{6,14},{7,15},{8,0},{9,1},... | collective-permute-start | bytes 2359304 | tf_op jit(solution)/shard_map/ppermute | solution.py:107
  460.2 83.6 %collective-permute-start.64 = (bf16[192,1024]{1,0:T(8,128)(2,1)}, bf16[192,1024]{1,0:T(8,128)(2,1)}, u32[]{:S(2)}, u32[]{:S(2)}) collective-permute-start(bf16[192,1024]{1,0:T(8,128)(2,1)} %slice.503), channel_id=1, source_target_pairs={{0,16},{1,17},{2,18},{3,19},{4,20},{5,21},{6,22},{7,23},{8,24},{9,... | collective-permute-start | bytes 1179656 | tf_op jit(solution)/shard_map/ppermute | solution.py:107
  460.9 45.7 %collective-permute-start.61 = (bf16[192,1024]{1,0:T(8,128)(2,1)S(1)}, bf16[192,1024]{1,0:T(8,128)(2,1)S(1)}, u32[]{:S(2)}, u32[]{:S(2)}) collective-permute-start(bf16[192,1024]{1,0:T(8,128)(2,1)S(1)} %slice.504), channel_id=1, source_target_pairs={{0,16},{1,17},{2,18},{3,19},{4,20},{5,21},{6,22},{7,23},{8,24},{9,... | collective-permute-start | bytes 1179656 | tf_op jit(solution)/shard_map/ppermute | solution.py:107
  489.6 56.4 %collective-permute-start.43 = (bf16[384,1536]{1,0:T(8,128)(2,1)S(1)}, bf16[384,1536]{1,0:T(8,128)(2,1)}, u32[]{:S(2)}, u32[]{:S(2)}) collective-permute-start(bf16[384,1536]{1,0:T(8,128)(2,1)S(1)} %slice.495), channel_id=1, source_target_pairs={{0,2},{1,3},{2,0},{3,1},{4,6},{5,7},{6,4},{7,5},{8,10},{9,11},{10,... | collective-permute-start | bytes 3538952 | tf_op jit(solution)/shard_map/ppermute | solution.py:107
  495.3 272.0 %collective-permute-start.38 = (bf16[384,1536]{1,0:T(8,128)(2,1)}, bf16[384,1536]{1,0:T(8,128)(2,1)}, u32[]{:S(2)}, u32[]{:S(2)}) collective-permute-start(bf16[384,1536]{1,0:T(8,128)(2,1)} %slice.496), channel_id=1, source_target_pairs={{0,2},{1,3},{2,0},{3,1},{4,6},{5,7},{6,4},{7,5},{8,10},{9,11},{10,... | collective-permute-start | bytes 3538952 | tf_op jit(solution)/shard_map/ppermute | solution.py:107
  625.9 95.8 %collective-permute-start.44 = (bf16[384,3072]{1,0:T(8,128)(2,1)S(1)}, bf16[384,3072]{1,0:T(8,128)(2,1)S(1)}, u32[]{:S(2)}, u32[]{:S(2)}) collective-permute-start(bf16[384,3072]{1,0:T(8,128)(2,1)S(1)} %convolution_convert_fusion.3), channel_id=1, source_target_pairs={{0,1},{1,0},{2,3},{3,2},{4,5},{5,4},{6,7},{7,6},{8,9},{9,8},{10,11... | collective-permute-start | bytes 7077896 | tf_op jit(solution)/shard_map/ppermute | solution.py:107
  640.7 80.9 %collective-permute-start.46 = (bf16[384,3072]{1,0:T(8,128)(2,1)S(1)}, bf16[384,3072]{1,0:T(8,128)(2,1)S(1)}, u32[]{:S(2)}, u32[]{:S(2)}) collective-permute-start(bf16[384,3072]{1,0:T(8,128)(2,1)S(1)} %add_convert_fusion), channel_id=1, source_target_pairs={{0,2},{1,3},{2,0},{3,1},{4,6},{5,7},{6,4},{7,5},{8,10},{9,11},{10,... | collective-permute-start | bytes 7077896 | tf_op jit(solution)/shard_map/ppermute | solution.py:107
  642.5 77.0 %collective-permute-start.52 = (bf16[384,1536]{1,0:T(8,128)(2,1)S(1)}, bf16[384,1536]{1,0:T(8,128)(2,1)S(1)}, u32[]{:S(2)}, u32[]{:S(2)}) collective-permute-start(bf16[384,1536]{1,0:T(8,128)(2,1)S(1)} %add_convert_fusion.3), channel_id=1, source_target_pairs={{0,2},{1,3},{2,0},{3,1},{4,6},{5,7},{6,4},{7,5},{8,10},{9,11},{10,... | collective-permute-start | bytes 3538952 | tf_op jit(solution)/shard_map/ppermute | solution.py:107
  723.0 43.4 %collective-permute-start.47 = (bf16[192,3072]{1,0:T(8,128)(2,1)S(1)}, bf16[192,3072]{1,0:T(8,128)(2,1)S(1)}, u32[]{:S(2)}, u32[]{:S(2)}) collective-permute-start(bf16[192,3072]{1,0:T(8,128)(2,1)S(1)} %slice.494), channel_id=1, source_target_pairs={{0,8},{1,9},{2,10},{3,11},{4,12},{5,13},{6,14},{7,15},{8,0},{9,1},... | collective-permute-start | bytes 3538952 | tf_op jit(solution)/shard_map/ppermute | solution.py:107
  (124 other events, 2425.2 us)
where the time goes:
time: 816 us; the launch traced here: 806 us
  waiting for transfers between devices  386 us (47%)
  matrix products  181 us (22%)
  local copies, waits for them, and re-layouts  104 us (13%)
  starting transfers between devices  59.2 us (7%)
  other arithmetic  43.3 us (5%)
  blocking collectives  29.6 us (4%)
    ppermute x65, waiting for transfers between devices, swap(): return lax.ppermute(array, AXES, [(i, i ^ mask) for i in range(world)])  386 us
    dot_general x16, matrix products, against(): lax.dot_general(left_side, right_side, (((1,), (1,)), ((), ())), preferre...  67.4 us
    dot_general x14, matrix products, product(): return jnp.dot(left_side, right_side, preferred_element_type=f32)  66.6 us
    ppermute x65, starting transfers between devices, swap(): return lax.ppermute(array, AXES, [(i, i ^ mask) for i in range(world)])  59.2 us
    unnamed x201, local copies, waits for them, and re-layouts  42.8 us
    dot_general x14, matrix products, across(): lax.dot_general(left_side, right_side, (((0,), (0,)), ((), ())), preferre...  36.2 us
    psum x1, blocking collectives, per_device(): second = lax.psum(second, 'tensor')  29.6 us
  transfers between devices with their start and end apart: 65, of which 26 were waited for; matrix products, arithmetic and copies ran while one was open for 35% of the time, Pallas kernels for 0%

commit v1 on v0

--- a/solution.py
+++ b/solution.py
@@ -308,7 +308,7 @@
         second = jnp.sum(
             gate_weight.astype(f32) * gate_grad + up_weight.astype(f32) * up_grad, axis=1
         )
-        second = lax.psum(second, "tensor")
+        second = jnp.sum(lax.all_gather(second, "tensor"), 0)
         second = lax.dynamic_slice(second, (t_i * shard,), (shard,))
         second_gain_grad = second / second_gain.astype(f32)
         return (

time: 816 us -> 817 us (level)
    psum x1 -> x0, blocking collectives: 29.6 us -> none  [per_device(): second = lax.psum(second, 'tensor')]
    unnamed x0 -> x1, blocking collectives: none -> 29.6 us
    unnamed x201 -> x210, local copies, waits for them, and re-layouts: 42.8 us -> 43.5 us
where the time goes in v1:
time: 817 us; the launch traced here: 807 us
  waiting for transfers between devices  386 us (47%)
  matrix products  181 us (22%)
  local copies, waits for them, and re-layouts  104 us (13%)
  starting transfers between devices  59.6 us (7%)
  other arithmetic  42.7 us (5%)
  blocking collectives  29.6 us (4%)
    ppermute x65, waiting for transfers between devices, swap(): return lax.ppermute(array, AXES, [(i, i ^ mask) for i in range(world)])  386 us
    dot_general x16, matrix products, against(): lax.dot_general(left_side, right_side, (((1,), (1,)), ((), ())), preferre...  67.4 us
    dot_general x14, matrix products, product(): return jnp.dot(left_side, right_side, preferred_element_type=f32)  66.6 us
    ppermute x65, starting transfers between devices, swap(): return lax.ppermute(array, AXES, [(i, i ^ mask) for i in range(world)])  59.6 us
    unnamed x210, local copies, waits for them, and re-layouts  43.5 us
    dot_general x14, matrix products, across(): lax.dot_general(left_side, right_side, (((0,), (0,)), ((), ())), preferre...  36.2 us
    unnamed x1, blocking collectives  29.6 us
  transfers between devices with their start and end apart: 65, of which 26 were waited for; matrix products, arithmetic and copies ran while one was open for 35% of the time, Pallas kernels for 0%

profile of v1, /device:TPU:0, one launch (start us, length us, event | category | flops | bytes accessed | tf_op | source)
XLA Modules:
  0.0 806.7 jit_solution(12888782083300831156)
XLA Ops:
  31.1 8.6 %collective-permute-done.4 = bf16[96,3200]{1,0:T(8,128)(2,1)S(1)} collective-permute-done((bf16[96,3200]{1,0:T(8,128)(2,1)S(1)}, bf16[96,3200]{1,0:T(8,128)(2,1)S(1)}, u32[]{:S(2)}, u32[]{:S(2)}) %collective-permute-start.4) | collective-permute-done | bytes 614432 | tf_op jit(solution)/shard_map/ppermute | solution.py:107
  41.0 27.5 %collective-permute-done.1 = bf16[96,3200]{1,0:T(8,128)(2,1)S(1)} collective-permute-done((bf16[96,3200]{1,0:T(8,128)(2,1)S(1)}, bf16[96,3200]{1,0:T(8,128)(2,1)S(1)}, u32[]{:S(2)}, u32[]{:S(2)}) %collective-permute-start.1) | collective-permute-done | bytes 614432 | tf_op jit(solution)/shard_map/ppermute | solution.py:107
  77.4 8.4 %collective-permute-done.3 = bf16[96,3200]{1,0:T(8,128)(2,1)S(1)} collective-permute-done((bf16[96,3200]{1,0:T(8,128)(2,1)S(1)}, bf16[96,3200]{1,0:T(8,128)(2,1)S(1)}, u32[]{:S(2)}, u32[]{:S(2)}) %collective-permute-start.3) | collective-permute-done | bytes 614432 | tf_op jit(solution)/shard_map/ppermute | solution.py:107
  89.6 13.0 %collective-permute-done.6 = bf16[96,3200]{1,0:T(8,128)(2,1)S(1)} collective-permute-done((bf16[96,3200]{1,0:T(8,128)(2,1)S(1)}, bf16[96,3200]{1,0:T(8,128)(2,1)S(1)}, u32[]{:S(2)}, u32[]{:S(2)}) %collective-permute-start.6) | collective-permute-done | bytes 614432 | tf_op jit(solution)/shard_map/ppermute | solution.py:107
  103.4 9.9 %collective-permute-done.7 = bf16[96,3200]{1,0:T(8,128)(2,1)S(1)} collective-permute-done((bf16[96,3200]{1,0:T(8,128)(2,1)S(1)}, bf16[96,3200]{1,0:T(8,128)(2,1)S(1)}, u32[]{:S(2)}, u32[]{:S(2)}) %collective-permute-start.7) | collective-permute-done | bytes 614432 | tf_op jit(solution)/shard_map/ppermute | solution.py:107
  142.6 7.3 collective-permute-done.34
  150.5 23.1 %collective-permute-done.23 = bf16[192,2048]{1,0:T(8,128)(2,1)S(1)} collective-permute-done((bf16[192,2048]{1,0:T(8,128)(2,1)}, bf16[192,2048]{1,0:T(8,128)(2,1)S(1)}, u32[]{:S(2)}, u32[]{:S(2)}) %collective-permute-start.23) | collective-permute-done | bytes 786464 | tf_op jit(solution)/shard_map/ppermute | solution.py:107
  255.3 18.8 %collective-permute-done.36 = bf16[192,1024]{1,0:T(8,128)(2,1)S(1)} collective-permute-done((bf16[192,1024]{1,0:T(8,128)(2,1)S(1)}, bf16[192,1024]{1,0:T(8,128)(2,1)S(1)}, u32[]{:S(2)}, u32[]{:S(2)}) %collective-permute-start.36) | collective-permute-done | bytes 393248 | tf_op jit(solution)/shard_map/ppermute | solution.py:107
  281.5 13.4 %collective-permute-done.28 = bf16[192,2048]{1,0:T(8,128)(2,1)S(1)} collective-permute-done((bf16[192,2048]{1,0:T(8,128)(2,1)}, bf16[192,2048]{1,0:T(8,128)(2,1)S(1)}, u32[]{:S(2)}, u32[]{:S(2)}) %collective-permute-start.28) | collective-permute-done | bytes 786464 | tf_op jit(solution)/shard_map/ppermute | solution.py:107
  296.3 13.2 %collective-permute-done.29 = bf16[192,2048]{1,0:T(8,128)(2,1)S(1)} collective-permute-done((bf16[192,2048]{1,0:T(8,128)(2,1)S(1)}, bf16[192,2048]{1,0:T(8,128)(2,1)S(1)}, u32[]{:S(2)}, u32[]{:S(2)}) %collective-permute-start.29) | collective-permute-done | bytes 786464 | tf_op jit(solution)/shard_map/ppermute | solution.py:107
  315.3 16.8 %fusion.176 = f32[1536,2048]{1,0:T(8,128)} fusion(bf16[1536,2048]{1,0:T(8,128)(2,1)S(1)} %copy-done.68, bf16[384,1536]{1,0:T(8,128)(2,1)S(1)} %collective-permute-done.22, bf16[384,1536]{1,0:T(8,128)(2,1)S(1)} %collective-permute-done.21, bf16[384,1536]{1,0:T(8,128)(2,1)S(1)} %collective-permute-done.20, bf16[384,1536]{1,0:T(8,128)(2,1)S(1)} %fusion.47), kind=kOutput, calls=%fused_computation.319 | convolution fusion | flops 9682550784 | bytes 23592960 | tf_op jit(solution)/shard_map/dot_general | solution.py:55
  332.1 15.0 %multiply_convert_fusion.1 = (bf16[1536,1024]{1,0:T(8,128)(2,1)S(1)}, bf16[1536,1024]{1,0:T(8,128)(2,1)}, bf16[1536,1024]{1,0:T(8,128)(2,1)}) fusion(f32[1536,2048]{1,0:T(8,128)} %fusion.176, bf16[1536,1024]{1,0:T(8,128)(2,1)} %constant_dynamic-update-slice_fusion.31, bf16[384,1536]{1,0:T(8,128)(2,1)} %copy-done.42, bf16[384,1536]{1,0:T(8,128)(2,1)} %copy-done.41, ...), kind=kOutput, calls=%fused_computation.19 | convolution fusion | flops 4875878400 | bytes 29884416 | tf_op jit(solution)/shard_map/dot_general | solution.py:55
  347.1 6.8 fusion.92
  361.1 15.1 %convolution_convert_fusion.1 = bf16[1536,1536]{1,0:T(8,128)(2,1)} fusion(bf16[1536,2048]{1,0:T(8,128)(2,1)} %constant_dynamic-update-slice_fusion.22, bf16[1536,1024]{1,0:T(8,128)(2,1)} %get-tuple-element.19, bf16[1536,1024]{1,0:T(8,128)(2,1)S(1)} %get-tuple-element.18), kind=kOutput, calls=%fused_computation.14 | convolution fusion | flops 9678618624 | bytes 17301504 | tf_op jit(solution)/shard_map/dot_general | solution.py:65
  380.6 7.4 convolution_convert_fusion
  397.3 28.0 %collective-permute-done.59 = bf16[768,1024]{1,0:T(8,128)(2,1)} collective-permute-done((bf16[768,1024]{1,0:T(8,128)(2,1)}, bf16[768,1024]{1,0:T(8,128)(2,1)}, u32[]{:S(2)}, u32[]{:S(2)}) %collective-permute-start.59) | collective-permute-done | bytes 1572896 | tf_op jit(solution)/shard_map/ppermute | solution.py:107
  431.0 24.9 %collective-permute-done.56 = bf16[768,1024]{1,0:T(8,128)(2,1)S(1)} collective-permute-done((bf16[768,1024]{1,0:T(8,128)(2,1)}, bf16[768,1024]{1,0:T(8,128)(2,1)S(1)}, u32[]{:S(2)}, u32[]{:S(2)}) %collective-permute-start.56) | collective-permute-done | bytes 1572896 | tf_op jit(solution)/shard_map/ppermute | solution.py:107
  464.9 22.8 %collective-permute-done.57 = bf16[384,1024]{1,0:T(8,128)(2,1)S(1)} collective-permute-done((bf16[384,1024]{1,0:T(8,128)(2,1)S(1)}, bf16[384,1024]{1,0:T(8,128)(2,1)S(1)}, u32[]{:S(2)}, u32[]{:S(2)}) %collective-permute-start.57) | collective-permute-done | bytes 786464 | tf_op jit(solution)/shard_map/ppermute | solution.py:107
  498.0 10.0 %collective-permute-done.61 = bf16[192,1024]{1,0:T(8,128)(2,1)S(1)} collective-permute-done((bf16[192,1024]{1,0:T(8,128)(2,1)S(1)}, bf16[192,1024]{1,0:T(8,128)(2,1)S(1)}, u32[]{:S(2)}, u32[]{:S(2)}) %collective-permute-start.61) | collective-permute-done | bytes 393248 | tf_op jit(solution)/shard_map/ppermute | solution.py:107
  513.8 29.6 %all-reduce.1 = f32[768]{0:T(1024)S(1)} all-reduce(f32[768]{0:T(1024)S(1)} %dynamic-update-slice), channel_id=2, replica_groups=mesh['dp'=8,'tensor'=4] {'tensor'}, use_global_device_ids=true, to_apply=%add.1 | all-reduce | flops 768 | bytes 6144
  650.8 69.7 %collective-permute-done.52 = bf16[384,1536]{1,0:T(8,128)(2,1)S(1)} collective-permute-done((bf16[384,1536]{1,0:T(8,128)(2,1)S(1)}, bf16[384,1536]{1,0:T(8,128)(2,1)S(1)}, u32[]{:S(2)}, u32[]{:S(2)}) %collective-permute-start.52) | collective-permute-done | bytes 1179680 | tf_op jit(solution)/shard_map/ppermute | solution.py:107
  740.2 27.2 %collective-permute-done.47 = bf16[192,3072]{1,0:T(8,128)(2,1)S(1)} collective-permute-done((bf16[192,3072]{1,0:T(8,128)(2,1)S(1)}, bf16[192,3072]{1,0:T(8,128)(2,1)S(1)}, u32[]{:S(2)}, u32[]{:S(2)}) %collective-permute-start.47) | collective-permute-done | bytes 1179680 | tf_op jit(solution)/shard_map/ppermute | solution.py:107
  774.6 20.6 %collective-permute-done.48 = bf16[96,3072]{1,0:T(8,128)(2,1)S(1)} collective-permute-done((bf16[96,3072]{1,0:T(8,128)(2,1)S(1)}, bf16[96,3072]{1,0:T(8,128)(2,1)S(1)}, u32[]{:S(2)}, u32[]{:S(2)}) %collective-permute-start.48) | collective-permute-done | bytes 589856 | tf_op jit(solution)/shard_map/ppermute | solution.py:107
  797.7 6.6 collective-permute-done.49
  (482 shorter events, 359.9 us)
Async XLA Ops:
  0.7 113.6 %collective-permute-start.30 = (bf16[192,1024]{1,0:T(8,128)(2,1)}, bf16[192,1024]{1,0:T(8,128)(2,1)}, u32[]{:S(2)}, u32[]{:S(2)}) collective-permute-start(bf16[192,1024]{1,0:T(8,128)(2,1)} %bitcast.153), channel_id=1, source_target_pairs={{0,16},{1,17},{2,18},{3,19},{4,20},{5,21},{6,22},{7,23},{8,24},{9,... | collective-permute-start | bytes 1179656 | tf_op jit(solution)/shard_map/ppermute | solution.py:107
  4.8 111.0 %collective-permute-start.31 = (bf16[192,1024]{1,0:T(8,128)(2,1)}, bf16[192,1024]{1,0:T(8,128)(2,1)}, u32[]{:S(2)}, u32[]{:S(2)}) collective-permute-start(bf16[192,1024]{1,0:T(8,128)(2,1)} %bitcast.154), channel_id=1, source_target_pairs={{0,8},{1,9},{2,10},{3,11},{4,12},{5,13},{6,14},{7,15},{8,0},{9,1},... | collective-permute-start | bytes 1179656 | tf_op jit(solution)/shard_map/ppermute | solution.py:107
  27.4 90.0 %collective-permute-start.11 = (bf16[96,1536]{1,0:T(8,128)(2,1)}, bf16[96,1536]{1,0:T(8,128)(2,1)S(1)}, u32[]{:S(2)}, u32[]{:S(2)}) collective-permute-start(bf16[96,1536]{1,0:T(8,128)(2,1)} %get-tuple-element.42), channel_id=1, source_target_pairs={{0,16},{1,17},{2,18},{3,19},{4,20},{5,21},{6,22},{7,23},{8,24},{9,... | collective-permute-start | bytes 884744 | tf_op jit(solution)/shard_map/ppermute | solution.py:107
  113.3 65.9 %collective-permute-start.8 = (bf16[384,3200]{1,0:T(8,128)(2,1)}, bf16[384,3200]{1,0:T(8,128)(2,1)}, u32[]{:S(2)}, u32[]{:S(2)}) collective-permute-start(bf16[384,3200]{1,0:T(8,128)(2,1)} %constant_dynamic-update-slice_fusion), channel_id=1, source_target_pairs={{0,1},{1,0},{2,3},{3,2},{4,5},{5,4},{6,7},{7,6},{8,9},{9,8},{10,11... | collective-permute-start | bytes 7372808 | tf_op jit(solution)/shard_map/ppermute | solution.py:107
  114.2 66.1 %collective-permute-start.9 = (bf16[384,3200]{1,0:T(8,128)(2,1)}, bf16[384,3200]{1,0:T(8,128)(2,1)}, u32[]{:S(2)}, u32[]{:S(2)}) collective-permute-start(bf16[384,3200]{1,0:T(8,128)(2,1)} %constant_dynamic-update-slice_fusion.5), channel_id=1, source_target_pairs={{0,1},{1,0},{2,3},{3,2},{4,5},{5,4},{6,7},{7,6},{8,9},{9,8},{10,11... | collective-permute-start | bytes 7372808 | tf_op jit(solution)/shard_map/ppermute | solution.py:107
  142.5 103.9 %collective-permute-start.24 = (bf16[192,2048]{1,0:T(8,128)(2,1)}, bf16[192,2048]{1,0:T(8,128)(2,1)}, u32[]{:S(2)}, u32[]{:S(2)}) collective-permute-start(bf16[192,2048]{1,0:T(8,128)(2,1)} %get-tuple-element.35), channel_id=1, source_target_pairs={{0,8},{1,9},{2,10},{3,11},{4,12},{5,13},{6,14},{7,15},{8,0},{9,1},... | collective-permute-start | bytes 2359304 | tf_op jit(solution)/shard_map/ppermute | solution.py:107
  173.5 74.5 %collective-permute-start.26 = (bf16[192,2048]{1,0:T(8,128)(2,1)}, bf16[192,2048]{1,0:T(8,128)(2,1)}, u32[]{:S(2)}, u32[]{:S(2)}) collective-permute-start(bf16[192,2048]{1,0:T(8,128)(2,1)} %get-tuple-element.35), channel_id=1, source_target_pairs={{0,4},{1,5},{2,6},{3,7},{4,0},{5,1},{6,2},{7,3},{8,12},{9,13},{10,... | collective-permute-start | bytes 2359304 | tf_op jit(solution)/shard_map/ppermute | solution.py:107
  176.0 100.4 %collective-permute-start.39 = (bf16[384,1536]{1,0:T(8,128)(2,1)}, bf16[384,1536]{1,0:T(8,128)(2,1)}, u32[]{:S(2)}, u32[]{:S(2)}) collective-permute-start(bf16[384,1536]{1,0:T(8,128)(2,1)} %fusion.57), channel_id=1, source_target_pairs={{0,2},{1,3},{2,0},{3,1},{4,6},{5,7},{6,4},{7,5},{8,10},{9,11},{10,... | collective-permute-start | bytes 3538952 | tf_op jit(solution)/shard_map/ppermute | solution.py:107
  179.3 58.2 %collective-permute-start.18 = (bf16[384,1536]{1,0:T(8,128)(2,1)}, bf16[384,1536]{1,0:T(8,128)(2,1)}, u32[]{:S(2)}, u32[]{:S(2)}) collective-permute-start(bf16[384,1536]{1,0:T(8,128)(2,1)} %constant_dynamic-update-slice_fusion.11), channel_id=1, source_target_pairs={{0,1},{1,0},{2,3},{3,2},{4,5},{5,4},{6,7},{7,6},{8,9},{9,8},{10,11... | collective-permute-start | bytes 3538952 | tf_op jit(solution)/shard_map/ppermute | solution.py:107
  180.4 59.7 %collective-permute-start.19 = (bf16[384,1536]{1,0:T(8,128)(2,1)}, bf16[384,1536]{1,0:T(8,128)(2,1)}, u32[]{:S(2)}, u32[]{:S(2)}) collective-permute-start(bf16[384,1536]{1,0:T(8,128)(2,1)} %constant_dynamic-update-slice_fusion.16), channel_id=1, source_target_pairs={{0,1},{1,0},{2,3},{3,2},{4,5},{5,4},{6,7},{7,6},{8,9},{9,8},{10,11... | collective-permute-start | bytes 3538952 | tf_op jit(solution)/shard_map/ppermute | solution.py:107
  250.9 44.0 %collective-permute-start.20 = (bf16[384,1536]{1,0:T(8,128)(2,1)S(1)}, bf16[384,1536]{1,0:T(8,128)(2,1)S(1)}, u32[]{:S(2)}, u32[]{:S(2)}) collective-permute-start(bf16[384,1536]{1,0:T(8,128)(2,1)S(1)} %fusion.47), channel_id=1, source_target_pairs={{0,2},{1,3},{2,0},{3,1},{4,6},{5,7},{6,4},{7,5},{8,10},{9,11},{10,... | collective-permute-start | bytes 3538952 | tf_op jit(solution)/shard_map/ppermute | solution.py:107
  359.6 65.7 %collective-permute-start.59 = (bf16[768,1024]{1,0:T(8,128)(2,1)}, bf16[768,1024]{1,0:T(8,128)(2,1)}, u32[]{:S(2)}, u32[]{:S(2)}) collective-permute-start(bf16[768,1024]{1,0:T(8,128)(2,1)} %fusion.89), channel_id=1, source_target_pairs={{0,4},{1,5},{2,6},{3,7},{4,0},{5,1},{6,2},{7,3},{8,12},{9,13},{10,... | collective-permute-start | bytes 4718600 | tf_op jit(solution)/shard_map/ppermute | solution.py:107
  380.0 75.8 %collective-permute-start.56 = (bf16[768,1024]{1,0:T(8,128)(2,1)}, bf16[768,1024]{1,0:T(8,128)(2,1)S(1)}, u32[]{:S(2)}, u32[]{:S(2)}) collective-permute-start(bf16[768,1024]{1,0:T(8,128)(2,1)} %fusion.86), channel_id=1, source_target_pairs={{0,4},{1,5},{2,6},{3,7},{4,0},{5,1},{6,2},{7,3},{8,12},{9,13},{10,... | collective-permute-start | bytes 4718600 | tf_op jit(solution)/shard_map/ppermute | solution.py:107
  388.1 100.2 %collective-permute-start.42 = (bf16[768,1536]{1,0:T(8,128)(2,1)S(1)}, bf16[768,1536]{1,0:T(8,128)(2,1)}, u32[]{:S(2)}, u32[]{:S(2)}) collective-permute-start(bf16[768,1536]{1,0:T(8,128)(2,1)S(1)} %slice.327), channel_id=1, source_target_pairs={{0,1},{1,0},{2,3},{3,2},{4,5},{5,4},{6,7},{7,6},{8,9},{9,8},{10,11... | collective-permute-start | bytes 7077896 | tf_op jit(solution)/shard_map/ppermute | solution.py:107
  388.4 104.6 %collective-permute-start.37 = (bf16[768,1536]{1,0:T(8,128)(2,1)S(1)}, bf16[768,1536]{1,0:T(8,128)(2,1)}, u32[]{:S(2)}, u32[]{:S(2)}) collective-permute-start(bf16[768,1536]{1,0:T(8,128)(2,1)S(1)} %slice.323), channel_id=1, source_target_pairs={{0,1},{1,0},{2,3},{3,2},{4,5},{5,4},{6,7},{7,6},{8,9},{9,8},{10,11... | collective-permute-start | bytes 7077896 | tf_op jit(solution)/shard_map/ppermute | solution.py:107
  395.9 64.5 %collective-permute-start.63 = (bf16[384,1024]{1,0:T(8,128)(2,1)S(1)}, bf16[384,1024]{1,0:T(8,128)(2,1)S(1)}, u32[]{:S(2)}, u32[]{:S(2)}) collective-permute-start(bf16[384,1024]{1,0:T(8,128)(2,1)S(1)} %slice.497), channel_id=1, source_target_pairs={{0,8},{1,9},{2,10},{3,11},{4,12},{5,13},{6,14},{7,15},{8,0},{9,1},... | collective-permute-start | bytes 2359304 | tf_op jit(solution)/shard_map/ppermute | solution.py:107
  461.5 83.2 %collective-permute-start.64 = (bf16[192,1024]{1,0:T(8,128)(2,1)}, bf16[192,1024]{1,0:T(8,128)(2,1)}, u32[]{:S(2)}, u32[]{:S(2)}) collective-permute-start(bf16[192,1024]{1,0:T(8,128)(2,1)} %slice.503), channel_id=1, source_target_pairs={{0,16},{1,17},{2,18},{3,19},{4,20},{5,21},{6,22},{7,23},{8,24},{9,... | collective-permute-start | bytes 1179656 | tf_op jit(solution)/shard_map/ppermute | solution.py:107
  462.3 45.7 %collective-permute-start.61 = (bf16[192,1024]{1,0:T(8,128)(2,1)S(1)}, bf16[192,1024]{1,0:T(8,128)(2,1)S(1)}, u32[]{:S(2)}, u32[]{:S(2)}) collective-permute-start(bf16[192,1024]{1,0:T(8,128)(2,1)S(1)} %slice.504), channel_id=1, source_target_pairs={{0,16},{1,17},{2,18},{3,19},{4,20},{5,21},{6,22},{7,23},{8,24},{9,... | collective-permute-start | bytes 1179656 | tf_op jit(solution)/shard_map/ppermute | solution.py:107
  490.8 56.1 %collective-permute-start.43 = (bf16[384,1536]{1,0:T(8,128)(2,1)S(1)}, bf16[384,1536]{1,0:T(8,128)(2,1)}, u32[]{:S(2)}, u32[]{:S(2)}) collective-permute-start(bf16[384,1536]{1,0:T(8,128)(2,1)S(1)} %slice.495), channel_id=1, source_target_pairs={{0,2},{1,3},{2,0},{3,1},{4,6},{5,7},{6,4},{7,5},{8,10},{9,11},{10,... | collective-permute-start | bytes 3538952 | tf_op jit(solution)/shard_map/ppermute | solution.py:107
  496.5 271.7 %collective-permute-start.38 = (bf16[384,1536]{1,0:T(8,128)(2,1)}, bf16[384,1536]{1,0:T(8,128)(2,1)}, u32[]{:S(2)}, u32[]{:S(2)}) collective-permute-start(bf16[384,1536]{1,0:T(8,128)(2,1)} %slice.496), channel_id=1, source_target_pairs={{0,2},{1,3},{2,0},{3,1},{4,6},{5,7},{6,4},{7,5},{8,10},{9,11},{10,... | collective-permute-start | bytes 3538952 | tf_op jit(solution)/shard_map/ppermute | solution.py:107
  626.9 95.7 %collective-permute-start.44 = (bf16[384,3072]{1,0:T(8,128)(2,1)S(1)}, bf16[384,3072]{1,0:T(8,128)(2,1)S(1)}, u32[]{:S(2)}, u32[]{:S(2)}) collective-permute-start(bf16[384,3072]{1,0:T(8,128)(2,1)S(1)} %convolution_convert_fusion.3), channel_id=1, source_target_pairs={{0,1},{1,0},{2,3},{3,2},{4,5},{5,4},{6,7},{7,6},{8,9},{9,8},{10,11... | collective-permute-start | bytes 7077896 | tf_op jit(solution)/shard_map/ppermute | solution.py:107
  641.7 80.9 %collective-permute-start.46 = (bf16[384,3072]{1,0:T(8,128)(2,1)S(1)}, bf16[384,3072]{1,0:T(8,128)(2,1)S(1)}, u32[]{:S(2)}, u32[]{:S(2)}) collective-permute-start(bf16[384,3072]{1,0:T(8,128)(2,1)S(1)} %add_convert_fusion), channel_id=1, source_target_pairs={{0,2},{1,3},{2,0},{3,1},{4,6},{5,7},{6,4},{7,5},{8,10},{9,11},{10,... | collective-permute-start | bytes 7077896 | tf_op jit(solution)/shard_map/ppermute | solution.py:107
  643.5 77.0 %collective-permute-start.52 = (bf16[384,1536]{1,0:T(8,128)(2,1)S(1)}, bf16[384,1536]{1,0:T(8,128)(2,1)S(1)}, u32[]{:S(2)}, u32[]{:S(2)}) collective-permute-start(bf16[384,1536]{1,0:T(8,128)(2,1)S(1)} %add_convert_fusion.3), channel_id=1, source_target_pairs={{0,2},{1,3},{2,0},{3,1},{4,6},{5,7},{6,4},{7,5},{8,10},{9,11},{10,... | collective-permute-start | bytes 3538952 | tf_op jit(solution)/shard_map/ppermute | solution.py:107
  723.9 43.5 %collective-permute-start.47 = (bf16[192,3072]{1,0:T(8,128)(2,1)S(1)}, bf16[192,3072]{1,0:T(8,128)(2,1)S(1)}, u32[]{:S(2)}, u32[]{:S(2)}) collective-permute-start(bf16[192,3072]{1,0:T(8,128)(2,1)S(1)} %slice.494), channel_id=1, source_target_pairs={{0,8},{1,9},{2,10},{3,11},{4,12},{5,13},{6,14},{7,15},{8,0},{9,1},... | collective-permute-start | bytes 3538952 | tf_op jit(solution)/shard_map/ppermute | solution.py:107
  (127 other events, 2542.0 us)
